TPU v7x, 32 devices: a whole 2x2x4 slice. The times are simulated.
32 devices in a mesh: gx: 8 (over y, x, core), gz: 4 (over z).
Axes of the slice: x: 2, y: 2, z: 4, core: 2. Of those that a mesh axis runs over, the one named last changes fastest.
Arguments:
- pressure_now: float32 [128, 128, 512], P('gz', 'gx'), may hold values from -6 to 6
- pressure_prev: float32 [128, 128, 512], P('gz', 'gx'), may hold values from -6 to 6
- adjoint_now: float32 [128, 128, 512], P('gz', 'gx'), may hold values from -6 to 6
- adjoint_prev: float32 [128, 128, 512], P('gz', 'gx'), may hold values from -6 to 6
- speed2: float32 [128, 128, 512], P('gz', 'gx'), may hold values from 0.05 to 0.32
- layer_state: float32 [4096, 64, 128], P(('gx', 'gz')), may hold values from -3 to 3
- layer_maps: float32 [8, 64, 64], replicated, as said below
- send_rows: int32 [32, 32, 4], P(('gx', 'gz')), may hold values from -1 to 2047, as said below
- slot_patch: int32 [4096], P(('gx', 'gz')), may hold values from 0 to 255
- patch_material: int32 [256], replicated, may hold values from 0 to 7
Outputs:
- pressure_out: float32 [128, 128, 512], P('gz', 'gx')
- adjoint_out: float32 [128, 128, 512], P('gz', 'gx')
- patch_gradient: float32 [256, 128], P(('gx', 'gz'))
Inputs may be any that keep to these rules, and one draw needn't show every extreme that they name: `send_rows`: each device's non-negative entries are distinct rows of its tile; -1 marks an unused entry; for one device every entry aimed at it is used. `layer_maps`: each material's matrix has diagonal entries from 0.5 to 0.9.
All inputs are finite; a program needn't handle non-finite values.
Results may differ from a plain program's by a relative error of at most 0.00016.
Values sent between devices are 32-bit elements; how exact they have to be, the bound alone decides.
A program may use at most 192 MiB of HBM per device.

v0:
```python
import jax
import jax.numpy as jnp
from jax import lax
from jax.sharding import PartitionSpec as P

STEPS = 4


KAPPA = 0.5
BETA = 0.3


def with_halo(block, sides, width):
    for axis, dim in sides:
        count = lax.axis_size(axis)
        forward = [(i, i + 1) for i in range(count - 1)]
        backward = [(target, source) for source, target in forward]
        low = lax.ppermute(
            lax.slice_in_dim(block, block.shape[dim] - width, None, axis=dim), axis, forward
        )
        high = lax.ppermute(lax.slice_in_dim(block, 0, width, axis=dim), axis, backward)
        block = jnp.concatenate([low, block, high], axis=dim)
    return block


def advance(fields, previous, speed2, padded):
    along = jnp.pad(fields, ((0, 0), (0, 0), (0, 0), (1, 1)))
    beside = padded[:, 2:, 1:-1, :] + padded[:, :-2, 1:-1, :]
    beside = beside + padded[:, 1:-1, 2:, :] + padded[:, 1:-1, :-2, :]
    beside = beside + along[:, :, :, 2:] + along[:, :, :, :-2]
    return 2.0 * fields - previous + speed2[None] * (beside - 6.0 * fields)


def pick_rows(fields, sources, width):
    batch = fields.shape[0]
    rows = fields.reshape(batch, -1, width)
    flat = sources.reshape(-1)
    picked = jnp.take(rows, jnp.maximum(flat, 0), axis=1)
    return jnp.where((flat >= 0)[None, :, None], picked, 0.0)


def layer_update(layer, maps, air):
    push = KAPPA * (air - layer[:, :, 0, :])
    fresh = jnp.einsum("bsij,bsjw->bsiw", maps, layer, precision=lax.Precision.HIGHEST)
    return fresh + maps[:, :, :, 0][:, :, :, None] * push[:, :, None, :]


def couple(fields, sources, picked, back):
    batch = fields.shape[0]
    width = picked.shape[-1]
    flat = sources.reshape(-1)
    total = fields.shape[1] * fields.shape[2] * fields.shape[3] // width
    delta = jnp.where((flat >= 0)[None, :, None], BETA * (back - picked), 0.0)
    target = jnp.where(flat >= 0, flat, total)
    coupling = jnp.zeros((batch, total, width), jnp.float32).at[:, target].add(delta, mode="drop")
    return coupling.reshape(fields.shape)


def body(
    pressure_now,
    pressure_prev,
    adjoint_now,
    adjoint_prev,
    speed2,
    layer_state,
    layer_maps,
    send_rows,
    slot_patch,
    patch_material,
):
    slots = layer_state.shape[0]
    width = layer_state.shape[2]
    devices = lax.axis_size(("gx", "gz"))
    sources = send_rows[0]
    cap = sources.shape[1]
    patches = patch_material.shape[0]
    materials = jnp.take(patch_material, slot_patch)
    forward_maps = jnp.take(layer_maps, materials, axis=0)
    adjoint_maps = jnp.swapaxes(forward_maps, 1, 2)
    owners = (slot_patch[:, None] == jnp.arange(patches, dtype=jnp.int32)[None, :]).astype(
        jnp.float32
    )

    def step_pair(fields, previous, layer, maps, halo_fn, out_fn, back_fn):
        batch = fields.shape[0]
        picked = pick_rows(fields, sources, width)
        air = out_fn(picked.reshape(batch, devices, cap, width)).reshape(batch, slots, width)
        fresh = layer_update(layer, maps, air)
        back = back_fn(fresh[:, :, 0, :].reshape(batch, devices, cap, width)).reshape(
            batch, devices * cap, width
        )
        padded = halo_fn(fields)
        following = advance(fields, previous, speed2, padded) + couple(
            fields, sources, picked, back
        )
        return (following, fresh)

    gradient = jnp.zeros((patches // devices, width), jnp.float32)
    summed = jnp.zeros((slots, width), jnp.float32)

    def halo_single(fields):
        return with_halo(fields, (("gx", 2), ("gz", 1)), 1)

    def out_single(picked):
        return lax.all_to_all(picked, ("gx", "gz"), split_axis=1, concat_axis=1, tiled=True)

    def back_single(rims):
        return lax.all_to_all(rims, ("gx", "gz"), split_axis=1, concat_axis=1, tiled=True)

    current, earlier, layer = (pressure_now[None], pressure_prev[None], layer_state[None])
    stored = []
    for step in range(STEPS):
        following, layer = step_pair(
            current, earlier, layer, forward_maps[None], halo_single, out_single, back_single
        )
        earlier, current = (current, following)
        stored.append(layer[0])
    pressure_out = current[0]
    current, earlier = (adjoint_now[None], adjoint_prev[None])
    layer = jnp.zeros_like(layer_state)[None]
    for step in range(STEPS):
        following, layer = step_pair(
            current, earlier, layer, adjoint_maps[None], halo_single, out_single, back_single
        )
        earlier, current = (current, following)
        gather_gradient = gradient
        gather_gradient = gather_gradient + lax.psum_scatter(
            jnp.einsum(
                "sp,sw->pw",
                owners,
                jnp.sum(stored[STEPS - 1 - step] * layer[0], axis=1),
                precision=lax.Precision.HIGHEST,
            ),
            ("gx", "gz"),
            scatter_dimension=0,
            tiled=True,
        )
        gradient, summed = (gather_gradient, summed)
    adjoint_out = current[0]
    return (pressure_out, adjoint_out, gradient)


def solution(mesh):
    in_specs = (
        P("gz", "gx", None),
        P("gz", "gx", None),
        P("gz", "gx", None),
        P("gz", "gx", None),
        P("gz", "gx", None),
        P(("gx", "gz"), None, None),
        P(),
        P(("gx", "gz"), None, None),
        P(("gx", "gz")),
        P(),
    )
    out_specs = (P("gz", "gx", None), P("gz", "gx", None), P(("gx", "gz"), None))
    return jax.shard_map(body, mesh=mesh, in_specs=in_specs, out_specs=out_specs, check_vma=False)
```

profile of v0, /device:TPU:0, one launch (start us, length us, event | category | flops | bytes accessed | tf_op | source)
XLA Modules:
  0.0 623.5 jit_solution(10675399623767171265)
XLA Ops:
  10.5 3.7 collective-permute-start.16
  17.4 5.1 collective-permute-start
  27.0 7.4 %all-to-all-start.8 = ((f32[1,32,4,128]{3,2,0,1:T(4,128)}), f32[1,32,4,128]{3,2,0,1:T(4,128)S(1)}, u32[]{:S(2)}, u32[]{:S(2)}) async-start(f32[1,32,4,128]{3,2,0,1:T(4,128)} %bitcast.58), calls=%async_computation.8 | async-start | bytes 131072 | tf_op jit(solution)/shard_map/all_to_all | solution.py:105
  38.1 2.8 gather_fusion.1
  40.9 10.5 %fusion.17 = f32[128,64,128]{2,1,0:T(8,128)} fusion(f32[128,64,64]{2,1,0:T(8,128)} %gather_fusion.1, pred[128]{0:T(512)(128)(4,1)S(1)} %get-tuple-element.8), kind=kOutput, calls=%fused_computation.49 | convolution fusion | flops 805830656 | bytes 6291584 | tf_op jit(solution)/shard_map/bsij,bsjw->bsiw/dot_general | solution.py:44
  53.9 10.3 %fusion.22 = f32[128,64,128]{2,1,0:T(8,128)} fusion(f32[128,64,128]{2,1,0:T(8,128)} %param.17, f32[128,64,64]{2,1,0:T(8,128)} %gather_fusion.1, pred[128]{0:T(512)(128)(4,1)S(1)} %get-tuple-element.8), kind=kOutput, calls=%fused_computation.54 | convolution fusion | flops 805830656 | bytes 10485888 | tf_op jit(solution)/shard_map/bsij,bsjw->bsiw/dot_general | solution.py:44
  68.4 3.0 copy.71
  75.1 5.2 collective-permute-start.19
  80.3 3.8 fusion.9
  86.9 13.6 %all-to-all-start.9 = ((f32[1,32,4,128]{3,2,0,1:T(4,128)}), f32[1,32,4,128]{3,2,0,1:T(4,128)S(1)}, u32[]{:S(2)}, u32[]{:S(2)}) async-start(f32[1,32,4,128]{3,2,0,1:T(4,128)} %bitcast.62), calls=%async_computation.9 | async-start | bytes 131072 | tf_op jit(solution)/shard_map/all_to_all | solution.py:108
  100.5 13.5 %fusion.8 = f32[128,64,128]{2,1,0:T(8,128)} fusion(f32[128,64,128]{2,1,0:T(8,128)} %fusion.17, f32[128,64,64]{2,1,0:T(8,128)} %gather_fusion.1, f32[128,128]{1,0:T(8,128)S(1)} %bitcast.242, f32[128,64]{1,0:T(8,128)S(1)} %bitcast.224, pred[128]{0:T(512)(128)(4,1)S(1)} %get-tuple-element.8), kind=kOutput, calls=%fused_computation.39 | convolution fusion | flops 807927808 | bytes 10584192 | tf_op jit(solution)/shard_map/bsij,bsjw->bsiw/dot_general | solution.py:44
  118.6 3.7 fusion.83
  127.1 5.7 all-to-all-start.10
  136.1 3.7 collective-permute-start.20
  142.1 3.8 fusion.11
  148.6 5.7 all-to-all-start.11
  157.1 5.2 collective-permute-start.23
  164.9 5.2 collective-permute-start.3
  170.0 2.4 scatter_custom_fusion.5
  172.4 2.4 reshape.379
  174.8 5.8 fusion.89
  185.0 3.0 collective-permute-start.24
  190.9 4.8 all-to-all-start.12
  195.7 13.5 %fusion.10 = f32[128,64,128]{2,1,0:T(8,128)} fusion(f32[128,64,128]{2,1,0:T(8,128)} %fusion.8, f32[128,64,64]{2,1,0:T(8,128)} %gather_fusion.1, f32[128,128]{1,0:T(8,128)S(1)} %bitcast.230, f32[128,64]{1,0:T(8,128)S(1)} %bitcast.226, pred[128]{0:T(512)(128)(4,1)S(1)} %get-tuple-element.8), kind=kOutput, calls=%fused_computation.41 | convolution fusion | flops 807927808 | bytes 10584192 | tf_op jit(solution)/shard_map/bsij,bsjw->bsiw/dot_general | solution.py:44
  211.2 5.2 collective-permute-start.27
  216.4 4.9 all-to-all-start
  222.4 3.8 fusion.13
  229.0 6.1 all-to-all-start.13
  236.3 10.4 %fusion.2 = f32[128,64,128]{2,1,0:T(8,128)} fusion(f32[128,64,128]{2,1,0:T(8,128)} %fusion.22, f32[128,64,64]{2,1,0:T(8,128)} %gather_fusion.1, f32[128,128]{1,0:T(8,128)S(1)} %bitcast.232, f32[128,64]{1,0:T(8,128)S(1)} %bitcast.216, pred[128]{0:T(512)(128)(4,1)S(1)} %get-tuple-element.8), kind=kOutput, calls=%fused_computation.33 | convolution fusion | flops 807927808 | bytes 10584192 | tf_op jit(solution)/shard_map/bsij,bsjw->bsiw/dot_general | solution.py:44
  250.7 6.1 all-to-all-start.1
  256.8 2.4 scatter_custom_fusion.6
  261.6 5.6 fusion.95
  274.0 2.7 fusion.58
  279.8 3.0 collective-permute-start.28
  282.8 2.5 gather_fusion.9
  286.6 4.6 collective-permute-start.4
  291.2 2.5 gather_fusion.3
  295.3 7.4 %all-to-all-start.2 = ((f32[1,32,4,128]{3,2,0,1:T(4,128)}), f32[1,32,4,128]{3,2,0,1:T(4,128)}, u32[]{:S(2)}, u32[]{:S(2)}) async-start(f32[1,32,4,128]{3,2,0,1:T(4,128)} %bitcast.21), calls=%async_computation.2 | async-start | bytes 131072 | tf_op jit(solution)/shard_map/all_to_all | solution.py:105
  305.5 5.2 collective-permute-start.31
  313.3 5.3 collective-permute-start.7
  319.8 3.8 fusion.5
  326.4 4.8 all-to-all-start.3
  331.2 10.2 %fusion.4 = f32[128,64,128]{2,1,0:T(8,128)} fusion(f32[128,64,128]{2,1,0:T(8,128)} %fusion.2, f32[128,64,64]{2,1,0:T(8,128)} %gather_fusion.1, f32[128,128]{1,0:T(8,128)S(1)} %bitcast.236, f32[128,64]{1,0:T(8,128)S(1)} %bitcast.219, pred[128]{0:T(512)(128)(4,1)S(1)} %get-tuple-element.8), kind=kOutput, calls=%fused_computation.35 | convolution fusion | flops 807927808 | bytes 10584192 | tf_op jit(solution)/shard_map/bsij,bsjw->bsiw/dot_general | solution.py:44
  341.4 6.0 all-to-all-start.14
  347.4 2.4 scatter_custom_fusion.1
  349.8 2.4 reshape.361
  358.7 3.6 collective-permute-start.8
  363.8 6.1 all-to-all-start.4
  374.4 5.2 collective-permute-start.11
  380.7 3.8 fusion.7
  387.2 5.4 all-to-all-start.5
  392.7 10.4 %fusion.6 = f32[128,64,128]{2,1,0:T(8,128)} fusion(f32[128,64,128]{2,1,0:T(8,128)} %fusion.4, f32[128,64,64]{2,1,0:T(8,128)} %gather_fusion.1, f32[128,128]{1,0:T(8,128)S(1)} %bitcast.239, f32[128,64]{1,0:T(8,128)S(1)} %bitcast.221, pred[128]{0:T(512)(128)(4,1)S(1)} %get-tuple-element.8), kind=kOutput, calls=%fused_computation.37 | convolution fusion | flops 807927808 | bytes 10584192 | tf_op jit(solution)/shard_map/bsij,bsjw->bsiw/dot_general | solution.py:44
  403.1 2.5 scatter_custom_fusion.2
  405.6 2.4 reshape.366
  408.0 3.2 fusion.70
  415.3 5.9 all-to-all-start.6
  424.6 3.8 collective-permute-start.12
  429.9 23.3 %multiply_reduce_fusion = (f32[128,128]{1,0:T(8,128)}, f32[128,128]{1,0:T(8,128)}, f32[128,128]{1,0:T(8,128)}, f32[128,128]{1,0:T(8,128)}, f32[1,128,64,128]{3,2,1,0:T(8,128)S(1)}, /*index=5*/f32[1,128,64,128]{3,2,1,0:T(8,128)}) fusion(f32[128,64,128]{2,1,0:T(8,128)} %fusion.22, f32[128,128]{1,0:T(8,128)} %bitcast.246, f32[128,64]{1,0:T(8,128)S(1)} %bitcast.228, ...), kind=kOutput, calls=%fused_computation.19 | convolution fusion | flops 833028096 | bytes 40697984 | tf_op jit(solution)/shard_map/bsij,bsjw->bsiw/dot_general | solution.py:44
  453.9 5.7 all-to-all-start.7
  467.2 4.5 collective-permute-start.15
  473.5 118.8 %all-reduce.11.cloned.1.call-done = f32[256,128]{1,0:T(8,128)} async-done(((f32[256,128]{1,0:T(8,128)}), f32[256,128]{1,0:T(8,128)}) %all-reduce.11.cloned.1.call-update) | async-done | bytes 131088
  593.6 3.8 all-to-all-start.15
  600.2 6.8 %fusion.77 = f32[32,16,512]{2,1,0:T(8,128)} fusion(f32[1,32,16,512]{3,2,1,0:T(8,128)} %reshape.371, f32[1,32,16,512]{3,2,1,0:T(8,128)} %fusion.70, f32[1,32,1,512]{3,2,1,0:T(1,128)} %collective-permute-done.12, f32[1,32,1,512]{3,2,1,0:T(1,128)} %collective-permute-done.13, f32[1,1,18,512]{3,2,1,0:T(8,128)S(1)} %collective-permute-done.15, ...), kind=kLoop, calls=%fused_computation.128 | loop fusion | flops 5242880 | bytes 5447680 | tf_op jit(solution)/shard_map/squeeze | solution.py:118
  609.9 6.5 %fusion.102 = f32[32,16,512]{2,1,0:T(8,128)} fusion(f32[1,32,16,512]{3,2,1,0:T(8,128)} %reshape.389, f32[1,32,16,512]{3,2,1,0:T(8,128)} %copy-done.14, f32[1,32,1,512]{3,2,1,0:T(1,128)S(1)} %copy-done.28, f32[1,32,1,512]{3,2,1,0:T(1,128)S(1)} %copy-done.26, f32[1,1,18,512]{3,2,1,0:T(8,128)} %collective-permute-done.31, ...), kind=kLoop, calls=%fused_computation.153 | loop fusion | flops 5242880 | bytes 5447680 | tf_op jit(solution)/shard_map/squeeze | solution.py:139
  (218 shorter events, 135.6 us)
Async XLA Ops:
  7.2 31.0 %copy-start = (f32[8,64,64]{2,1,0:T(8,128)S(1)}, f32[8,64,64]{2,1,0:T(8,128)}, u32[]{:S(2)}) copy-start(f32[8,64,64]{2,1,0:T(8,128)} %param.18) | copy-start | bytes 393220
  9.2 63.3 %collective-permute-start.17 = (f32[1,32,1,512]{3,2,1,0:T(1,128)}, f32[1,32,1,512]{3,2,1,0:T(1,128)}, u32[]{:S(2)}, u32[]{:S(2)}) collective-permute-start(f32[1,32,1,512]{3,2,1,0:T(1,128)} %get-tuple-element.34), channel_id=1, source_target_pairs={{4,0},{8,4},{12,8},{16,12},{20,16},{24,20},{28,24},{5,1},{9,5},{13... | collective-permute-start | bytes 196616 | tf_op jit(solution)/shard_map/ppermute | solution.py:21
  10.5 62.0 %collective-permute-start.16 = (f32[1,32,1,512]{3,2,1,0:T(1,128)}, f32[1,32,1,512]{3,2,1,0:T(1,128)}, u32[]{:S(2)}, u32[]{:S(2)}) collective-permute-start(f32[1,32,1,512]{3,2,1,0:T(1,128)} %get-tuple-element.35), channel_id=1, source_target_pairs={{0,4},{4,8},{8,12},{12,16},{16,20},{20,24},{24,28},{1,5},{5,9},{9,... | collective-permute-start | bytes 196616 | tf_op jit(solution)/shard_map/ppermute | solution.py:18
  16.1 146.2 %collective-permute-start.1 = (f32[1,32,1,512]{3,2,1,0:T(1,128)}, f32[1,32,1,512]{3,2,1,0:T(1,128)S(1)}, u32[]{:S(2)}, u32[]{:S(2)}) collective-permute-start(f32[1,32,1,512]{3,2,1,0:T(1,128)} %get-tuple-element.42), channel_id=1, source_target_pairs={{4,0},{8,4},{12,8},{16,12},{20,16},{24,20},{28,24},{5,1},{9,5},{13... | collective-permute-start | bytes 196616 | tf_op jit(solution)/shard_map/ppermute | solution.py:21
  17.4 144.9 %collective-permute-start = (f32[1,32,1,512]{3,2,1,0:T(1,128)}, f32[1,32,1,512]{3,2,1,0:T(1,128)}, u32[]{:S(2)}, u32[]{:S(2)}) collective-permute-start(f32[1,32,1,512]{3,2,1,0:T(1,128)} %get-tuple-element.43), channel_id=1, source_target_pairs={{0,4},{4,8},{8,12},{12,16},{16,20},{20,24},{24,28},{1,5},{5,9},{9,... | collective-permute-start | bytes 196616 | tf_op jit(solution)/shard_map/ppermute | solution.py:18
  27.0 53.3 %all-to-all-start.8 = ((f32[1,32,4,128]{3,2,0,1:T(4,128)}), f32[1,32,4,128]{3,2,0,1:T(4,128)S(1)}, u32[]{:S(2)}, u32[]{:S(2)}) async-start(f32[1,32,4,128]{3,2,0,1:T(4,128)} %bitcast.58), calls=%async_computation.8 | async-start | bytes 131072 | tf_op jit(solution)/shard_map/all_to_all | solution.py:105
  40.9 10.5 %copy-start.2 = (f32[128,64,64]{2,1,0:T(8,128)S(1)}, f32[128,64,64]{2,1,0:T(8,128)}, u32[]{:S(2)}) copy-start(f32[128,64,64]{2,1,0:T(8,128)} %gather_fusion.1) | copy-start | bytes 6291460
  53.8 10.3 %copy-start.3 = (f32[128,64,64]{2,1,0:T(8,128)S(1)}, f32[128,64,64]{2,1,0:T(8,128)}, u32[]{:S(2)}) copy-start(f32[128,64,64]{2,1,0:T(8,128)} %gather_fusion.1) | copy-start | bytes 6291460
  73.8 44.7 %collective-permute-start.18 = (f32[1,1,18,512]{3,2,1,0:T(8,128)}, f32[1,1,18,512]{3,2,1,0:T(8,128)}, u32[]{:S(2)}, u32[]{:S(2)}) collective-permute-start(f32[1,1,18,512]{3,2,1,0:T(8,128)} %get-tuple-element.18), channel_id=1, source_target_pairs={{1,0},{2,1},{3,2},{5,4},{6,5},{7,6},{9,8},{10,9},{11,10},{13,12},{... | collective-permute-start | bytes 110600 | tf_op jit(solution)/shard_map/ppermute | solution.py:21
  75.1 43.4 %collective-permute-start.19 = (f32[1,1,18,512]{3,2,1,0:T(8,128)}, f32[1,1,18,512]{3,2,1,0:T(8,128)}, u32[]{:S(2)}, u32[]{:S(2)}) collective-permute-start(f32[1,1,18,512]{3,2,1,0:T(8,128)} %get-tuple-element.19), channel_id=1, source_target_pairs={{0,1},{1,2},{2,3},{4,5},{5,6},{6,7},{8,9},{9,10},{10,11},{12,13},{... | collective-permute-start | bytes 110600 | tf_op jit(solution)/shard_map/ppermute | solution.py:18
  80.3 20.1 %copy-start.22 = (f32[1,32,4,128]{3,2,0,1:T(4,128)}, f32[1,32,4,128]{3,2,0,1:T(4,128)S(1)}, u32[]{:S(2)}) copy-start(f32[1,32,4,128]{3,2,0,1:T(4,128)S(1)} %broadcast_multiply_fusion) | copy-start | bytes 196612
  86.9 27.1 %all-to-all-start.9 = ((f32[1,32,4,128]{3,2,0,1:T(4,128)}), f32[1,32,4,128]{3,2,0,1:T(4,128)S(1)}, u32[]{:S(2)}, u32[]{:S(2)}) async-start(f32[1,32,4,128]{3,2,0,1:T(4,128)} %bitcast.62), calls=%async_computation.9 | async-start | bytes 131072 | tf_op jit(solution)/shard_map/all_to_all | solution.py:108
  100.4 18.1 %copy-start.4 = (f32[32,16,512]{2,1,0:T(8,128)S(1)}, f32[32,16,512]{2,1,0:T(8,128)}, u32[]{:S(2)}) copy-start(f32[32,16,512]{2,1,0:T(8,128)} %param.16) | copy-start | bytes 3145732
  127.1 13.2 %all-to-all-start.10 = ((f32[1,32,4,128]{3,2,0,1:T(4,128)}), f32[1,32,4,128]{3,2,0,1:T(4,128)S(1)}, u32[]{:S(2)}, u32[]{:S(2)}) async-start(f32[1,32,4,128]{3,2,0,1:T(4,128)} %bitcast.67), calls=%async_computation.10 | async-start | bytes 131072 | tf_op jit(solution)/shard_map/all_to_all | solution.py:105
  134.8 19.6 %collective-permute-start.21 = (f32[1,32,1,512]{3,2,1,0:T(1,128)}, f32[1,32,1,512]{3,2,1,0:T(1,128)S(1)}, u32[]{:S(2)}, u32[]{:S(2)}) collective-permute-start(f32[1,32,1,512]{3,2,1,0:T(1,128)} %get-tuple-element.32), channel_id=1, source_target_pairs={{4,0},{8,4},{12,8},{16,12},{20,16},{24,20},{28,24},{5,1},{9,5},{13... | collective-permute-start | bytes 196616 | tf_op jit(solution)/shard_map/ppermute | solution.py:21
  136.1 18.3 %collective-permute-start.20 = (f32[1,32,1,512]{3,2,1,0:T(1,128)}, f32[1,32,1,512]{3,2,1,0:T(1,128)}, u32[]{:S(2)}, u32[]{:S(2)}) collective-permute-start(f32[1,32,1,512]{3,2,1,0:T(1,128)} %get-tuple-element.33), channel_id=1, source_target_pairs={{0,4},{4,8},{8,12},{12,16},{16,20},{20,24},{24,28},{1,5},{5,9},{9,... | collective-permute-start | bytes 196616 | tf_op jit(solution)/shard_map/ppermute | solution.py:18
  148.6 21.4 %all-to-all-start.11 = ((f32[1,32,4,128]{3,2,0,1:T(4,128)}), f32[1,32,4,128]{3,2,0,1:T(4,128)}, u32[]{:S(2)}, u32[]{:S(2)}) async-start(f32[1,32,4,128]{3,2,0,1:T(4,128)} %bitcast.254), calls=%async_computation.11 | async-start | bytes 131072 | tf_op jit(solution)/shard_map/all_to_all | solution.py:108
  155.8 19.0 %collective-permute-start.22 = (f32[1,1,18,512]{3,2,1,0:T(8,128)}, f32[1,1,18,512]{3,2,1,0:T(8,128)}, u32[]{:S(2)}, u32[]{:S(2)}) collective-permute-start(f32[1,1,18,512]{3,2,1,0:T(8,128)} %get-tuple-element.16), channel_id=1, source_target_pairs={{1,0},{2,1},{3,2},{5,4},{6,5},{7,6},{9,8},{10,9},{11,10},{13,12},{... | collective-permute-start | bytes 110600 | tf_op jit(solution)/shard_map/ppermute | solution.py:21
  157.1 17.7 %collective-permute-start.23 = (f32[1,1,18,512]{3,2,1,0:T(8,128)}, f32[1,1,18,512]{3,2,1,0:T(8,128)}, u32[]{:S(2)}, u32[]{:S(2)}) collective-permute-start(f32[1,1,18,512]{3,2,1,0:T(8,128)} %get-tuple-element.17), channel_id=1, source_target_pairs={{0,1},{1,2},{2,3},{4,5},{5,6},{6,7},{8,9},{9,10},{10,11},{12,13},{... | collective-permute-start | bytes 110600 | tf_op jit(solution)/shard_map/ppermute | solution.py:18
  163.6 110.4 %collective-permute-start.2 = (f32[1,1,18,512]{3,2,1,0:T(8,128)}, f32[1,1,18,512]{3,2,1,0:T(8,128)}, u32[]{:S(2)}, u32[]{:S(2)}) collective-permute-start(f32[1,1,18,512]{3,2,1,0:T(8,128)} %get-tuple-element.26), channel_id=1, source_target_pairs={{1,0},{2,1},{3,2},{5,4},{6,5},{7,6},{9,8},{10,9},{11,10},{13,12},{... | collective-permute-start | bytes 110600 | tf_op jit(solution)/shard_map/ppermute | solution.py:21
  164.9 109.1 %collective-permute-start.3 = (f32[1,1,18,512]{3,2,1,0:T(8,128)}, f32[1,1,18,512]{3,2,1,0:T(8,128)}, u32[]{:S(2)}, u32[]{:S(2)}) collective-permute-start(f32[1,1,18,512]{3,2,1,0:T(8,128)} %get-tuple-element.27), channel_id=1, source_target_pairs={{0,1},{1,2},{2,3},{4,5},{5,6},{6,7},{8,9},{9,10},{10,11},{12,13},{... | collective-permute-start | bytes 110600 | tf_op jit(solution)/shard_map/ppermute | solution.py:18
  183.7 25.6 %collective-permute-start.25 = (f32[1,32,1,512]{3,2,1,0:T(1,128)}, f32[1,32,1,512]{3,2,1,0:T(1,128)S(1)}, u32[]{:S(2)}, u32[]{:S(2)}) collective-permute-start(f32[1,32,1,512]{3,2,1,0:T(1,128)} %get-tuple-element.30), channel_id=1, source_target_pairs={{4,0},{8,4},{12,8},{16,12},{20,16},{24,20},{28,24},{5,1},{9,5},{13... | collective-permute-start | bytes 196616 | tf_op jit(solution)/shard_map/ppermute | solution.py:21
  185.0 24.3 %collective-permute-start.24 = (f32[1,32,1,512]{3,2,1,0:T(1,128)}, f32[1,32,1,512]{3,2,1,0:T(1,128)S(1)}, u32[]{:S(2)}, u32[]{:S(2)}) collective-permute-start(f32[1,32,1,512]{3,2,1,0:T(1,128)} %get-tuple-element.31), channel_id=1, source_target_pairs={{0,4},{4,8},{8,12},{12,16},{16,20},{20,24},{24,28},{1,5},{5,9},{9,... | collective-permute-start | bytes 196616 | tf_op jit(solution)/shard_map/ppermute | solution.py:18
  190.9 25.5 %all-to-all-start.12 = ((f32[1,32,4,128]{3,2,0,1:T(4,128)}), f32[1,32,4,128]{3,2,0,1:T(4,128)S(1)}, u32[]{:S(2)}, u32[]{:S(2)}) async-start(f32[1,32,4,128]{3,2,0,1:T(4,128)} %bitcast.77), calls=%async_computation.12 | async-start | bytes 131072 | tf_op jit(solution)/shard_map/all_to_all | solution.py:105
  195.7 13.6 %copy-start.10 = (f32[1,32,16,512]{3,2,1,0:T(8,128)S(1)}, f32[1,32,16,512]{3,2,1,0:T(8,128)}, u32[]{:S(2)}) copy-start(f32[1,32,16,512]{3,2,1,0:T(8,128)} %copy-done.9) | copy-start | bytes 3145732
  209.2 12.0 %copy-start.29 = (f32[1,32,1,512]{3,2,1,0:T(1,128)}, f32[1,32,1,512]{3,2,1,0:T(1,128)S(1)}, u32[]{:S(2)}) copy-start(f32[1,32,1,512]{3,2,1,0:T(1,128)S(1)} %collective-permute-done.24) | copy-start | bytes 196612
  209.9 51.7 %collective-permute-start.26 = (f32[1,1,18,512]{3,2,1,0:T(8,128)}, f32[1,1,18,512]{3,2,1,0:T(8,128)}, u32[]{:S(2)}, u32[]{:S(2)}) collective-permute-start(f32[1,1,18,512]{3,2,1,0:T(8,128)} %get-tuple-element.14), channel_id=1, source_target_pairs={{1,0},{2,1},{3,2},{5,4},{6,5},{7,6},{9,8},{10,9},{11,10},{13,12},{... | collective-permute-start | bytes 110600 | tf_op jit(solution)/shard_map/ppermute | solution.py:21
  211.2 50.4 %collective-permute-start.27 = (f32[1,1,18,512]{3,2,1,0:T(8,128)}, f32[1,1,18,512]{3,2,1,0:T(8,128)}, u32[]{:S(2)}, u32[]{:S(2)}) collective-permute-start(f32[1,1,18,512]{3,2,1,0:T(8,128)} %get-tuple-element.15), channel_id=1, source_target_pairs={{0,1},{1,2},{2,3},{4,5},{5,6},{6,7},{8,9},{9,10},{10,11},{12,13},{... | collective-permute-start | bytes 110600 | tf_op jit(solution)/shard_map/ppermute | solution.py:18
  216.4 12.6 %all-to-all-start = ((f32[1,32,4,128]{3,2,0,1:T(4,128)}), f32[1,32,4,128]{3,2,0,1:T(4,128)S(1)}, u32[]{:S(2)}, u32[]{:S(2)}) async-start(f32[1,32,4,128]{3,2,0,1:T(4,128)} %bitcast.10), calls=%async_computation | async-start | bytes 131072 | tf_op jit(solution)/shard_map/all_to_all | solution.py:105
  229.0 21.7 %all-to-all-start.13 = ((f32[1,32,4,128]{3,2,0,1:T(4,128)}), f32[1,32,4,128]{3,2,0,1:T(4,128)}, u32[]{:S(2)}, u32[]{:S(2)}) async-start(f32[1,32,4,128]{3,2,0,1:T(4,128)} %bitcast.82), calls=%async_computation.13 | async-start | bytes 131072 | tf_op jit(solution)/shard_map/all_to_all | solution.py:108
  236.3 10.4 %copy-start.5 = (f32[128,64,128]{2,1,0:T(8,128)S(1)}, f32[128,64,128]{2,1,0:T(8,128)}, u32[]{:S(2)}) copy-start(f32[128,64,128]{2,1,0:T(8,128)} %fusion.22) | copy-start | bytes 12582916
  246.7 14.9 %copy-start.8 = (f32[1,32,16,512]{3,2,1,0:T(8,128)S(1)}, f32[1,32,16,512]{3,2,1,0:T(8,128)}, u32[]{:S(2)}) copy-start(f32[1,32,16,512]{3,2,1,0:T(8,128)} %fusion.83) | copy-start | bytes 3145732
  250.7 20.4 %all-to-all-start.1 = ((f32[1,32,4,128]{3,2,0,1:T(4,128)}), f32[1,32,4,128]{3,2,0,1:T(4,128)}, u32[]{:S(2)}, u32[]{:S(2)}) async-start(f32[1,32,4,128]{3,2,0,1:T(4,128)} %bitcast.255), calls=%async_computation.1 | async-start | bytes 131072 | tf_op jit(solution)/shard_map/all_to_all | solution.py:108
  278.5 24.2 %collective-permute-start.29 = (f32[1,32,1,512]{3,2,1,0:T(1,128)}, f32[1,32,1,512]{3,2,1,0:T(1,128)S(1)}, u32[]{:S(2)}, u32[]{:S(2)}) collective-permute-start(f32[1,32,1,512]{3,2,1,0:T(1,128)} %get-tuple-element.28), channel_id=1, source_target_pairs={{4,0},{8,4},{12,8},{16,12},{20,16},{24,20},{28,24},{5,1},{9,5},{13... | collective-permute-start | bytes 196616 | tf_op jit(solution)/shard_map/ppermute | solution.py:21
  279.8 22.9 %collective-permute-start.28 = (f32[1,32,1,512]{3,2,1,0:T(1,128)}, f32[1,32,1,512]{3,2,1,0:T(1,128)S(1)}, u32[]{:S(2)}, u32[]{:S(2)}) collective-permute-start(f32[1,32,1,512]{3,2,1,0:T(1,128)} %get-tuple-element.29), channel_id=1, source_target_pairs={{0,4},{4,8},{8,12},{12,16},{16,20},{20,24},{24,28},{1,5},{5,9},{9,... | collective-permute-start | bytes 196616 | tf_op jit(solution)/shard_map/ppermute | solution.py:18
  285.3 25.4 %collective-permute-start.5 = (f32[1,32,1,512]{3,2,1,0:T(1,128)}, f32[1,32,1,512]{3,2,1,0:T(1,128)}, u32[]{:S(2)}, u32[]{:S(2)}) collective-permute-start(f32[1,32,1,512]{3,2,1,0:T(1,128)} %get-tuple-element.40), channel_id=1, source_target_pairs={{4,0},{8,4},{12,8},{16,12},{20,16},{24,20},{28,24},{5,1},{9,5},{13... | collective-permute-start | bytes 196616 | tf_op jit(solution)/shard_map/ppermute | solution.py:21
  286.6 24.1 %collective-permute-start.4 = (f32[1,32,1,512]{3,2,1,0:T(1,128)}, f32[1,32,1,512]{3,2,1,0:T(1,128)}, u32[]{:S(2)}, u32[]{:S(2)}) collective-permute-start(f32[1,32,1,512]{3,2,1,0:T(1,128)} %get-tuple-element.41), channel_id=1, source_target_pairs={{0,4},{4,8},{8,12},{12,16},{16,20},{20,24},{24,28},{1,5},{5,9},{9,... | collective-permute-start | bytes 196616 | tf_op jit(solution)/shard_map/ppermute | solution.py:18
  295.3 23.4 %all-to-all-start.2 = ((f32[1,32,4,128]{3,2,0,1:T(4,128)}), f32[1,32,4,128]{3,2,0,1:T(4,128)}, u32[]{:S(2)}, u32[]{:S(2)}) async-start(f32[1,32,4,128]{3,2,0,1:T(4,128)} %bitcast.21), calls=%async_computation.2 | async-start | bytes 131072 | tf_op jit(solution)/shard_map/all_to_all | solution.py:105
  302.7 16.0 %copy-start.25 = (f32[1,32,1,512]{3,2,1,0:T(1,128)}, f32[1,32,1,512]{3,2,1,0:T(1,128)S(1)}, u32[]{:S(2)}) copy-start(f32[1,32,1,512]{3,2,1,0:T(1,128)S(1)} %collective-permute-done.29) | copy-start | bytes 196612
  302.7 20.9 %copy-start.27 = (f32[1,32,1,512]{3,2,1,0:T(1,128)}, f32[1,32,1,512]{3,2,1,0:T(1,128)S(1)}, u32[]{:S(2)}) copy-start(f32[1,32,1,512]{3,2,1,0:T(1,128)S(1)} %collective-permute-done.28) | copy-start | bytes 196612
  304.2 305.7 %collective-permute-start.30 = (f32[1,1,18,512]{3,2,1,0:T(8,128)}, f32[1,1,18,512]{3,2,1,0:T(8,128)}, u32[]{:S(2)}, u32[]{:S(2)}) collective-permute-start(f32[1,1,18,512]{3,2,1,0:T(8,128)} %get-tuple-element.12), channel_id=1, source_target_pairs={{1,0},{2,1},{3,2},{5,4},{6,5},{7,6},{9,8},{10,9},{11,10},{13,12},{... | collective-permute-start | bytes 110600 | tf_op jit(solution)/shard_map/ppermute | solution.py:21
  305.5 304.4 %collective-permute-start.31 = (f32[1,1,18,512]{3,2,1,0:T(8,128)}, f32[1,1,18,512]{3,2,1,0:T(8,128)}, u32[]{:S(2)}, u32[]{:S(2)}) collective-permute-start(f32[1,1,18,512]{3,2,1,0:T(8,128)} %get-tuple-element.13), channel_id=1, source_target_pairs={{0,1},{1,2},{2,3},{4,5},{5,6},{6,7},{8,9},{9,10},{10,11},{12,13},{... | collective-permute-start | bytes 110600 | tf_op jit(solution)/shard_map/ppermute | solution.py:18
  312.0 40.2 %collective-permute-start.6 = (f32[1,1,18,512]{3,2,1,0:T(8,128)}, f32[1,1,18,512]{3,2,1,0:T(8,128)}, u32[]{:S(2)}, u32[]{:S(2)}) collective-permute-start(f32[1,1,18,512]{3,2,1,0:T(8,128)} %get-tuple-element.24), channel_id=1, source_target_pairs={{1,0},{2,1},{3,2},{5,4},{6,5},{7,6},{9,8},{10,9},{11,10},{13,12},{... | collective-permute-start | bytes 110600 | tf_op jit(solution)/shard_map/ppermute | solution.py:21
  313.3 38.9 %collective-permute-start.7 = (f32[1,1,18,512]{3,2,1,0:T(8,128)}, f32[1,1,18,512]{3,2,1,0:T(8,128)}, u32[]{:S(2)}, u32[]{:S(2)}) collective-permute-start(f32[1,1,18,512]{3,2,1,0:T(8,128)} %get-tuple-element.25), channel_id=1, source_target_pairs={{0,1},{1,2},{2,3},{4,5},{5,6},{6,7},{8,9},{9,10},{10,11},{12,13},{... | collective-permute-start | bytes 110600 | tf_op jit(solution)/shard_map/ppermute | solution.py:18
  326.4 15.0 %all-to-all-start.3 = ((f32[1,32,4,128]{3,2,0,1:T(4,128)}), f32[1,32,4,128]{3,2,0,1:T(4,128)S(1)}, u32[]{:S(2)}, u32[]{:S(2)}) async-start(f32[1,32,4,128]{3,2,0,1:T(4,128)} %bitcast.256), calls=%async_computation.3 | async-start | bytes 131072 | tf_op jit(solution)/shard_map/all_to_all | solution.py:108
  341.4 22.3 %all-to-all-start.14 = ((f32[1,32,4,128]{3,2,0,1:T(4,128)}), f32[1,32,4,128]{3,2,0,1:T(4,128)}, u32[]{:S(2)}, u32[]{:S(2)}) async-start(f32[1,32,4,128]{3,2,0,1:T(4,128)} %bitcast.87), calls=%async_computation.14 | async-start | bytes 131072 | tf_op jit(solution)/shard_map/all_to_all | solution.py:105
  357.4 14.2 %collective-permute-start.9 = (f32[1,32,1,512]{3,2,1,0:T(1,128)}, f32[1,32,1,512]{3,2,1,0:T(1,128)}, u32[]{:S(2)}, u32[]{:S(2)}) collective-permute-start(f32[1,32,1,512]{3,2,1,0:T(1,128)} %get-tuple-element.38), channel_id=1, source_target_pairs={{4,0},{8,4},{12,8},{16,12},{20,16},{24,20},{28,24},{5,1},{9,5},{13... | collective-permute-start | bytes 196616 | tf_op jit(solution)/shard_map/ppermute | solution.py:21
  358.7 12.9 %collective-permute-start.8 = (f32[1,32,1,512]{3,2,1,0:T(1,128)}, f32[1,32,1,512]{3,2,1,0:T(1,128)}, u32[]{:S(2)}, u32[]{:S(2)}) collective-permute-start(f32[1,32,1,512]{3,2,1,0:T(1,128)} %get-tuple-element.39), channel_id=1, source_target_pairs={{0,4},{4,8},{8,12},{12,16},{16,20},{20,24},{24,28},{1,5},{5,9},{9,... | collective-permute-start | bytes 196616 | tf_op jit(solution)/shard_map/ppermute | solution.py:18
  363.0 16.5 %copy-start.24 = (f32[128,128]{1,0:T(8,128)}, f32[128,128]{1,0:T(8,128)S(1)}, u32[]{:S(2)}) copy-start(f32[128,128]{1,0:T(8,128)S(1)} %gather_fusion.4) | copy-start | bytes 196612
  363.8 15.8 %all-to-all-start.4 = ((f32[1,32,4,128]{3,2,0,1:T(4,128)}), f32[1,32,4,128]{3,2,0,1:T(4,128)S(1)}, u32[]{:S(2)}, u32[]{:S(2)}) async-start(f32[1,32,4,128]{3,2,0,1:T(4,128)} %bitcast.31), calls=%async_computation.4 | async-start | bytes 131072 | tf_op jit(solution)/shard_map/all_to_all | solution.py:105
  373.1 34.9 %collective-permute-start.10 = (f32[1,1,18,512]{3,2,1,0:T(8,128)}, f32[1,1,18,512]{3,2,1,0:T(8,128)}, u32[]{:S(2)}, u32[]{:S(2)}) collective-permute-start(f32[1,1,18,512]{3,2,1,0:T(8,128)} %get-tuple-element.22), channel_id=1, source_target_pairs={{1,0},{2,1},{3,2},{5,4},{6,5},{7,6},{9,8},{10,9},{11,10},{13,12},{... | collective-permute-start | bytes 110600 | tf_op jit(solution)/shard_map/ppermute | solution.py:21
  374.4 33.6 %collective-permute-start.11 = (f32[1,1,18,512]{3,2,1,0:T(8,128)}, f32[1,1,18,512]{3,2,1,0:T(8,128)}, u32[]{:S(2)}, u32[]{:S(2)}) collective-permute-start(f32[1,1,18,512]{3,2,1,0:T(8,128)} %get-tuple-element.23), channel_id=1, source_target_pairs={{0,1},{1,2},{2,3},{4,5},{5,6},{6,7},{8,9},{9,10},{10,11},{12,13},{... | collective-permute-start | bytes 110600 | tf_op jit(solution)/shard_map/ppermute | solution.py:18
  387.2 15.8 %all-to-all-start.5 = ((f32[1,32,4,128]{3,2,0,1:T(4,128)}), f32[1,32,4,128]{3,2,0,1:T(4,128)}, u32[]{:S(2)}, u32[]{:S(2)}) async-start(f32[1,32,4,128]{3,2,0,1:T(4,128)} %bitcast.36), calls=%async_computation.5 | async-start | bytes 131072 | tf_op jit(solution)/shard_map/all_to_all | solution.py:108
  392.7 15.3 %copy-start.13 = (f32[1,32,16,512]{3,2,1,0:T(8,128)S(1)}, f32[1,32,16,512]{3,2,1,0:T(8,128)}, u32[]{:S(2)}) copy-start(f32[1,32,16,512]{3,2,1,0:T(8,128)} %copy-done.12) | copy-start | bytes 3145732
  415.3 13.4 %all-to-all-start.6 = ((f32[1,32,4,128]{3,2,0,1:T(4,128)}), f32[1,32,4,128]{3,2,0,1:T(4,128)S(1)}, u32[]{:S(2)}, u32[]{:S(2)}) async-start(f32[1,32,4,128]{3,2,0,1:T(4,128)} %bitcast.41), calls=%async_computation.6 | async-start | bytes 131072 | tf_op jit(solution)/shard_map/all_to_all | solution.py:105
  423.3 41.9 %collective-permute-start.13 = (f32[1,32,1,512]{3,2,1,0:T(1,128)}, f32[1,32,1,512]{3,2,1,0:T(1,128)}, u32[]{:S(2)}, u32[]{:S(2)}) collective-permute-start(f32[1,32,1,512]{3,2,1,0:T(1,128)} %get-tuple-element.36), channel_id=1, source_target_pairs={{4,0},{8,4},{12,8},{16,12},{20,16},{24,20},{28,24},{5,1},{9,5},{13... | collective-permute-start | bytes 196616 | tf_op jit(solution)/shard_map/ppermute | solution.py:21
  424.6 40.7 %collective-permute-start.12 = (f32[1,32,1,512]{3,2,1,0:T(1,128)}, f32[1,32,1,512]{3,2,1,0:T(1,128)}, u32[]{:S(2)}, u32[]{:S(2)}) collective-permute-start(f32[1,32,1,512]{3,2,1,0:T(1,128)} %get-tuple-element.37), channel_id=1, source_target_pairs={{0,4},{4,8},{8,12},{12,16},{16,20},{20,24},{24,28},{1,5},{5,9},{9,... | collective-permute-start | bytes 196616 | tf_op jit(solution)/shard_map/ppermute | solution.py:18
  429.9 29.8 %copy-start.31 = (s32[128]{0:T(128)S(1)}, s32[128]{0:T(128)}, u32[]{:S(2)}) copy-start(s32[128]{0:T(128)} %param.20) | copy-start | bytes 1540
  429.9 35.3 %copy-start.15 = (f32[1,32,16,512]{3,2,1,0:T(8,128)S(1)}, f32[1,32,16,512]{3,2,1,0:T(8,128)}, u32[]{:S(2)}) copy-start(f32[1,32,16,512]{3,2,1,0:T(8,128)} %fusion.70) | copy-start | bytes 3145732
  453.9 139.7 %all-to-all-start.7 = ((f32[1,32,4,128]{3,2,0,1:T(4,128)}), f32[1,32,4,128]{3,2,0,1:T(4,128)S(1)}, u32[]{:S(2)}, u32[]{:S(2)}) async-start(f32[1,32,4,128]{3,2,0,1:T(4,128)} %bitcast.46), calls=%async_computation.7 | async-start | bytes 131072 | tf_op jit(solution)/shard_map/all_to_all | solution.py:108
  459.7 132.7 %all-reduce.11.cloned.1.call-start = ((), (), s32[]{:S(2)}) async-start(), calls=%async_computation.16 | async-start | bytes 262144
  465.9 134.3 %collective-permute-start.14 = (f32[1,1,18,512]{3,2,1,0:T(8,128)S(1)}, f32[1,1,18,512]{3,2,1,0:T(8,128)S(1)}, u32[]{:S(2)}, u32[]{:S(2)}) collective-permute-start(f32[1,1,18,512]{3,2,1,0:T(8,128)S(1)} %get-tuple-element.20), channel_id=1, source_target_pairs={{1,0},{2,1},{3,2},{5,4},{6,5},{7,6},{9,8},{10,9},{11,10},{13,12},{... | collective-permute-start | bytes 110600 | tf_op jit(solution)/shard_map/ppermute | solution.py:21
  467.2 133.0 %collective-permute-start.15 = (f32[1,1,18,512]{3,2,1,0:T(8,128)S(1)}, f32[1,1,18,512]{3,2,1,0:T(8,128)S(1)}, u32[]{:S(2)}, u32[]{:S(2)}) collective-permute-start(f32[1,1,18,512]{3,2,1,0:T(8,128)S(1)} %get-tuple-element.21), channel_id=1, source_target_pairs={{0,1},{1,2},{2,3},{4,5},{5,6},{6,7},{8,9},{9,10},{10,11},{12,13},{... | collective-permute-start | bytes 110600 | tf_op jit(solution)/shard_map/ppermute | solution.py:18
  593.6 13.4 %all-to-all-start.15 = ((f32[1,32,4,128]{3,2,0,1:T(4,128)}), f32[1,32,4,128]{3,2,0,1:T(4,128)}, u32[]{:S(2)}, u32[]{:S(2)}) async-start(f32[1,32,4,128]{3,2,0,1:T(4,128)} %bitcast.92), calls=%async_computation.15 | async-start | bytes 131072 | tf_op jit(solution)/shard_map/all_to_all | solution.py:108
  (17 other events, 67.0 us)
Sparse Core Ops, SparseCore 0:
  466.6 125.7 all-reduce.10
where the time goes:
time: 633 us; the launch traced here: 623 us
  starting transfers between devices  191 us (30%)
  waiting for transfers between devices  120 us (19%)
  matrix products  108 us (17%)
  other arithmetic  107 us (17%)
  local copies, waits for them, and re-layouts  82.2 us (13%)
  between operations  15.1 us (2%)
    unnamed x2, waiting for transfers between devices  119 us
    dot_general x8, matrix products, layer_update(): jnp.einsum('bsij,bsjw->bsiw', maps, layer, precision=lax.Precision.HIGHEST)  102 us
    ppermute x16, starting transfers between devices, with_halo(): lax.ppermute(lax.slice_in_dim(block, block.shape[dim] - width, None, axis...  71.4 us
    all_to_all x8, starting transfers between devices, back_single(): lax.all_to_all(rims, ('gx', 'gz'), split_axis=1, concat_axis=1, tiled=True)  51.2 us
    all_to_all x8, starting transfers between devices, out_single(): lax.all_to_all(picked, ('gx', 'gz'), split_axis=1, concat_axis=1, tiled=T...  48.1 us
    add x6, other arithmetic, step_pair(): advance(fields, previous, speed2, padded)  23.2 us
    ppermute x16, starting transfers between devices, with_halo(): lax.ppermute(lax.slice_in_dim(block, 0, width, axis=dim), axis, backward)  20.5 us
    add x6, other arithmetic, layer_update(): return fresh + maps[:, :, :, 0][:, :, :, None] * push[:, :, None, :]  20.5 us
  transfers between devices with their start and end apart: 49, of which 3 were waited for; matrix products, arithmetic and copies ran while one was open for 43% of the time, Pallas kernels for 0%

commit v1 on v0

v1 whole, which is shorter than its diff:
```python
import functools

import jax
import jax.numpy as jnp
from jax import lax
from jax.experimental import pallas as pl
from jax.experimental.pallas import tpu as pltpu
from jax.sharding import PartitionSpec as P

STEPS = 4
KAPPA = 0.5
BETA = 0.3
ROWS = 2 * STEPS + 1
LANES = 128


def project_kernel(block, slot_patch, patch_material, maps, state, out, table, info):
    mats, depth, _ = maps.shape
    lane = lax.broadcasted_iota(jnp.int32, (1, depth), 1)
    halve = jnp.where(lane == 0, 1.0 - KAPPA, 1.0)
    row8 = lax.broadcasted_iota(jnp.int32, (8, LANES), 0)
    lane8 = lax.broadcasted_iota(jnp.int32, (8, LANES), 1)

    @pl.when(pl.program_id(0) == 0)
    def _():
        @pl.loop(0, mats)
        def _(m):
            full = maps[m]
            v = full[0:1, :]
            h = jnp.zeros_like(v)
            surface, inner = [], []
            for n in range(STEPS):
                dv = v * halve
                surface.append(dv)
                pair = jnp.concatenate([dv, v + h] + [jnp.zeros_like(v)] * 6, axis=0)
                got = jnp.dot(
                    pair, full, precision=lax.Precision.HIGHEST,
                    preferred_element_type=jnp.float32,
                )
                v = got[0:1]
                h = got[1:2] * halve
                inner.append(h)
            rows = jnp.concatenate(surface + inner, axis=0)
            table[m] = rows
            first = rows[:, 0:1] / (1.0 - KAPPA)
            info[m] = jnp.sum(jnp.where(row8 == lane8, first, 0.0), axis=0, keepdims=True)

    base = pl.program_id(0) * block
    lane1 = lax.broadcasted_iota(jnp.int32, (1, LANES), 1)

    for i in range(block):
        patch = slot_patch[base + i]
        mat = patch_material[patch]
        got = jnp.dot(
            table[mat], state[i], precision=lax.Precision.HIGHEST,
            preferred_element_type=jnp.float32,
        )
        for n in range(2 * STEPS):
            out[n, i : i + 1, :] = got[n : n + 1]
        patches = jnp.full((1, LANES), patch, jnp.int32).astype(jnp.float32)
        out[2 * STEPS, i : i + 1, :] = jnp.where(lane1 == ROWS - 1, patches, info[mat])


def project(slot_patch, patch_material, maps, state):
    slots, depth, width = state.shape
    mats = maps.shape[0]
    block = 16
    return pl.pallas_call(
        functools.partial(project_kernel, block),
        out_shape=jax.ShapeDtypeStruct((ROWS, slots, width), jnp.float32),
        grid_spec=pltpu.PrefetchScalarGridSpec(
            num_scalar_prefetch=2,
            grid=(slots // block,),
            in_specs=[
                pl.BlockSpec((mats, depth, depth), lambda i, *_: (0, 0, 0)),
                pl.BlockSpec((block, depth, width), lambda i, *_: (i, 0, 0)),
            ],
            out_specs=pl.BlockSpec((ROWS, block, width), lambda i, *_: (0, i, 0)),
            scratch_shapes=[
                pltpu.VMEM((mats, 2 * STEPS, depth), jnp.float32),
                pltpu.VMEM((mats, 1, width), jnp.float32),
            ],
        ),
    )(slot_patch, patch_material, maps, state)


def wave_kernel(
    nx, nz,
    p_now, p_prev, a_now, a_prev, speed2, src_lane, src_column, relay,
    p_out, a_out, corr,
    p_mid, a_mid, spread, pick, couple, hist,
    x_send, x_recv, z_recv, send_sem, recv_sem,
):
    cz, cx, ny = speed2.shape
    slots = relay.shape[1]
    blocks = ny // LANES
    gx, gz = lax.axis_index("gx"), lax.axis_index("gz")
    exists = [gx > 0, gx < nx - 1, gz > 0, gz < nz - 1]
    target = [(gx - 1, gz), (gx + 1, gz), (gx, gz - 1), (gx, gz + 1)]

    barrier = pltpu.get_barrier_semaphore()
    for d in range(4):
        @pl.when(exists[d])
        def _(d=d):
            pl.semaphore_signal(
                barrier, inc=1, device_id=target[d], device_id_type=pl.DeviceIdType.MESH
            )
    pl.semaphore_wait(barrier, sum(peer.astype(jnp.int32) for peer in exists))

    now = (p_now, a_now)
    prev = (p_prev, a_prev)
    mid = (p_mid, a_mid)
    outs = (p_out, a_out)

    def halo_copy(field, step, d, source):
        if d < 2:
            ref, dst = x_send.at[step, field, d], x_recv.at[step, field, 1 - d]
        else:
            ref = source.at[0 if d == 2 else cz - 1]
            dst = z_recv.at[step, field, 3 - d]
        return pltpu.make_async_remote_copy(
            src_ref=ref, dst_ref=dst,
            send_sem=send_sem.at[step, field, d],
            recv_sem=recv_sem.at[step, field, d ^ 1],
            device_id=target[d], device_id_type=pl.DeviceIdType.MESH,
        )

    def start_halo(field, step, source):
        for d in range(4):
            @pl.when(exists[d])
            def _(d=d):
                halo_copy(field, step, d, source).start()

    def wait_recv(field, step, source):
        for d in range(4):
            @pl.when(exists[d])
            def _(d=d):
                side = x_recv.at[step, field, d] if d < 2 else z_recv.at[step, field, d - 2]
                pltpu.make_async_remote_copy(
                    src_ref=side, dst_ref=side,
                    send_sem=send_sem.at[step, field, d],
                    recv_sem=recv_sem.at[step, field, d],
                    device_id=target[d], device_id_type=pl.DeviceIdType.MESH,
                ).wait_recv()

    def wait_send(field, step, source):
        for d in range(4):
            @pl.when(exists[d])
            def _(d=d):
                halo_copy(field, step, d, source).wait_send()

    for field in range(2):
        @pl.loop(0, cz)
        def _(z, field=field):
            x_send[0, field, 0, pl.ds(z, 1), :] = now[field][z, 0:1, :]
            x_send[0, field, 1, pl.ds(z, 1), :] = now[field][z, cx - 1 : cx, :]
        start_halo(field, 0, now[field])

    for d in range(4):
        @pl.when(jnp.logical_not(exists[d]))
        def _(d=d):
            for step in range(STEPS):
                for field in range(2):
                    if d < 2:
                        x_recv[step, field, d] = jnp.zeros((cz, ny), jnp.float32)
                    else:
                        z_recv[step, field, d - 2] = jnp.zeros((cx, ny), jnp.float32)

    lanes = src_lane[...]
    xrow = lax.broadcasted_iota(jnp.int32, (cx, slots), 0)

    @pl.loop(0, cz)
    def _(z):
        for rb in range(blocks):
            row = z * (cx * blocks) + xrow * blocks + rb
            hit = jnp.where(row == lanes, 1.0, 0.0).astype(jnp.bfloat16)
            spread[rb, pl.ds(pl.multiple_of(z * cx, cx), cx), :] = jnp.concatenate([hit, hit], axis=1)

    lane_row = lax.broadcasted_iota(jnp.int32, (slots, cz * cx), 1) * blocks
    column = src_column[...]
    for rb in range(blocks):
        pick[rb] = jnp.where(lane_row + rb == column, 1.0, 0.0).astype(jnp.bfloat16)

    def gather(source, field, step):
        picked = jnp.zeros((slots, LANES), jnp.float32)
        for rb in range(blocks):
            value = source[:, :, rb * LANES : (rb + 1) * LANES].reshape(cz * cx, LANES)
            high = value.astype(jnp.bfloat16)
            low = (value - high.astype(jnp.float32)).astype(jnp.bfloat16)
            for part in (high, low):
                picked = picked + jnp.dot(pick[rb], part, preferred_element_type=jnp.float32)
        hist[field, step] = picked

    def coef(n):
        return relay[ROWS - 1, :, n : n + 1]

    row_id = lax.broadcasted_iota(jnp.int32, (cx, ny), 0)
    lane_id = lax.broadcasted_iota(jnp.int32, (cx, ny), 1)

    for step in range(STEPS):
        for field in range(2):
            current = (now, mid, outs, mid)[step][field]
            earlier = (prev, now, mid, outs)[step][field]
            result = (mid, outs, mid, outs)[step][field]
            last = step == STEPS - 1

            gather(current, field, step)
            back = relay[step] if field == 0 else jnp.zeros((slots, LANES), jnp.float32)
            for t in range(step + 1):
                back = back + KAPPA * coef(step - t) * hist[field, t]
            delta = BETA * (back - hist[field, step])
            high = delta.astype(jnp.bfloat16)
            low = (delta - high.astype(jnp.float32)).astype(jnp.bfloat16)
            both = jnp.concatenate([high, low], axis=0)

            @pl.loop(0, blocks)
            def _(rb):
                couple[rb] = jnp.dot(spread[rb], both, preferred_element_type=jnp.float32)

            wait_recv(field, step, current)
            if step > 0:
                wait_send(field, step - 1, earlier)

            def plane(z, down, up):
                f = current[z]
                at = pl.multiple_of(z * cx, cx) if not isinstance(z, int) else z * cx
                lo = x_recv[step, field, 0, pl.ds(z, 1), :]
                hi = x_recv[step, field, 1, pl.ds(z, 1), :]
                west = jnp.where(row_id == 0, lo, pltpu.roll(f, 1, 0))
                east = jnp.where(row_id == cx - 1, hi, pltpu.roll(f, cx - 1, 0))
                south = jnp.where(lane_id == 0, 0.0, pltpu.roll(f, 1, 1))
                north = jnp.where(lane_id == ny - 1, 0.0, pltpu.roll(f, ny - 1, 1))
                beside = (down + up) + (west + east) + (south + north)
                extra = jnp.concatenate([couple[rb, pl.ds(at, cx), :] for rb in range(blocks)], axis=1)
                new = 2.0 * f - earlier[z] + speed2[z] * (beside - 6.0 * f) + extra
                result[z] = new
                if not last:
                    x_send[step + 1, field, 0, pl.ds(z, 1), :] = new[0:1]
                    x_send[step + 1, field, 1, pl.ds(z, 1), :] = new[cx - 1 : cx]

            plane(0, z_recv[step, field, 0], current[1])
            plane(cz - 1, current[cz - 2], z_recv[step, field, 1])

            @pl.loop(1, cz - 1)
            def _(z):
                plane(z, current[z - 1], current[z + 1])

            if last:
                wait_send(field, step, current)
            else:
                start_halo(field, step + 1, result)

    total = jnp.zeros((slots, LANES), jnp.float32)
    for t in range(STEPS):
        inner = relay[2 * STEPS - 1 - t]
        for other in range(STEPS - t):
            inner = inner + KAPPA * coef(STEPS + STEPS - 1 - t - other) * hist[0, other]
        total = total + KAPPA * hist[1, t] * inner
    corr[...] = total


def wave(nx, nz, p_now, p_prev, a_now, a_prev, speed2, src, relay):
    cz, cx, ny = speed2.shape
    slots = relay.shape[1]
    f32 = jnp.float32
    vmem = pl.BlockSpec(memory_space=pltpu.VMEM)
    return pl.pallas_call(
        functools.partial(wave_kernel, nx, nz),
        out_shape=(
            jax.ShapeDtypeStruct((cz, cx, ny), f32),
            jax.ShapeDtypeStruct((cz, cx, ny), f32),
            jax.ShapeDtypeStruct((slots, LANES), f32),
        ),
        in_specs=[vmem] * 8,
        out_specs=(vmem, vmem, vmem),
        scratch_shapes=[
            pltpu.VMEM((cz, cx, ny), f32),
            pltpu.VMEM((cz, cx, ny), f32),
            pltpu.VMEM((ny // LANES, cz * cx, 2 * slots), jnp.bfloat16),
            pltpu.VMEM((ny // LANES, slots, cz * cx), jnp.bfloat16),
            pltpu.VMEM((ny // LANES, cz * cx, LANES), f32),
            pltpu.VMEM((2, STEPS, slots, LANES), f32),
            pltpu.VMEM((STEPS, 2, 2, cz, ny), f32),
            pltpu.VMEM((STEPS, 2, 2, cz, ny), f32),
            pltpu.VMEM((STEPS, 2, 2, cx, ny), f32),
            pltpu.SemaphoreType.DMA((STEPS, 2, 4)),
            pltpu.SemaphoreType.DMA((STEPS, 2, 4)),
        ],
        compiler_params=pltpu.CompilerParams(
            collective_id=0, has_side_effects=True, vmem_limit_bytes=50 * 1024 * 1024
        ),
    )(p_now, p_prev, a_now, a_prev, speed2, src.reshape(1, slots), src.reshape(slots, 1), relay)


def body(
    nx, nz, pressure_now, pressure_prev, adjoint_now, adjoint_prev, speed2,
    layer_state, layer_maps, send_rows, slot_patch, patch_material,
):
    slots, _, width = layer_state.shape
    devices = nx * nz
    patches = patch_material.shape[0]
    cap = send_rows.shape[2]
    axes = ("gx", "gz")
    rows = project(slot_patch, patch_material, layer_maps, layer_state)
    relay = lax.all_to_all(
        rows.reshape(ROWS, devices, cap, width), axes, split_axis=1, concat_axis=1, tiled=True
    ).reshape(ROWS, slots, width)
    pressure_out, adjoint_out, corr = wave(
        nx, nz, pressure_now, pressure_prev, adjoint_now, adjoint_prev, speed2,
        send_rows.reshape(-1), relay,
    )
    patch = relay[ROWS - 1, :, ROWS - 1].astype(jnp.int32)
    owners = (patch[:, None] == jnp.arange(patches, dtype=jnp.int32)[None, :]).astype(jnp.float32)
    local = jnp.einsum("sp,sw->pw", owners, corr, precision=lax.Precision.HIGHEST)
    gradient = lax.psum_scatter(local, axes, scatter_dimension=0, tiled=True)
    return pressure_out, adjoint_out, gradient


def solution(mesh):
    in_specs = (
        P("gz", "gx", None),
        P("gz", "gx", None),
        P("gz", "gx", None),
        P("gz", "gx", None),
        P("gz", "gx", None),
        P(("gx", "gz"), None, None),
        P(),
        P(("gx", "gz"), None, None),
        P(("gx", "gz")),
        P(),
    )
    out_specs = (P("gz", "gx", None), P("gz", "gx", None), P(("gx", "gz"), None))
    return jax.shard_map(
        functools.partial(body, mesh.shape["gx"], mesh.shape["gz"]),
        mesh=mesh, in_specs=in_specs, out_specs=out_specs, check_vma=False,
    )
```

time: 633 us -> 225 us (0.36); the launches traced: 623 us -> 224 us
  starting transfers between devices: 191 us -> 7.37 us
  matrix products: 108 us -> 1.01 us
  other arithmetic: 107 us -> 0.17 us
  local copies, waits for them, and re-layouts: 82.2 us -> 5.58 us
  Pallas kernels: 0 us -> 56.1 us
  waiting for transfers between devices: 120 us -> 140 us
    dot_general x12 -> x1, matrix products: 108 us -> 1.01 us  [body(): jnp.einsum('sp,sw->pw', owners, corr, precision=lax.Precision.HIGHEST)]
    all_to_all x16 -> x1, starting transfers between devices: 99.3 us -> 7.32 us  [body(): lax.all_to_all(rows.reshape(ROWS, devices, cap, width), axes, split_axis=...]
    ppermute x32 -> x0, starting transfers between devices: 92 us -> none  [the longest x16 71.4 us: with_halo(): lax.ppermute(lax.slice_in_dim(block, block.shape[dim] - width, None, axis...]
    pallas_call x0 -> x2, Pallas kernels: none -> 56.1 us  [the longest x1 41.4 us: wave(): pl.pallas_call(functools.partial(wave_kernel, nx, nz), out_shape=(jax.Sha...]
    add x12 -> x0, other arithmetic: 43.7 us -> none  [the longest x6 23.2 us: step_pair(): advance(fields, previous, speed2, padded)]
    slice x17 -> x0, local copies, waits for them, and re-layouts: 18.6 us -> none  [the longest x8 10.9 us: with_halo(): lax.slice_in_dim(block, 0, width, axis=dim)]
    scatter-add x8 -> x0, other arithmetic: 17 us -> none  [couple(): jnp.zeros((batch, total, width), jnp.float32).at[:, target]]
    gather x10 -> x0, local copies, waits for them, and re-layouts: 16.2 us -> none  [the longest x8 11.8 us: pick_rows(): picked = jnp.take(rows, jnp.maximum(flat, 0), axis=1)]
  transfers between devices with their start and end apart: 49 -> 2, of which waited for: 3 -> 2; matrix products, arithmetic and copies ran while one was open for 43% -> 0% of each run, Pallas kernels for 0% -> 0%
where the time goes in v1:
time: 225 us; the launch traced here: 224 us
  waiting for transfers between devices  140 us (62%)
  Pallas kernels  56.1 us (25%)
  between operations  14.1 us (6%)
  starting transfers between devices  7.37 us (3%)
  local copies, waits for them, and re-layouts  5.58 us (2%)
    unnamed x2, waiting for transfers between devices  125 us
    pallas_call x1, Pallas kernels, wave(): pl.pallas_call(functools.partial(wave_kernel, nx, nz), out_shape=(jax.Sha...  41.4 us
    all_to_all x1, waiting for transfers between devices, body(): lax.all_to_all(rows.reshape(ROWS, devices, cap, width), axes, split_axis=...  15.2 us
    pallas_call x1, Pallas kernels, project(): pl.pallas_call(functools.partial(project_kernel, block), out_shape=jax.Sh...  14.6 us
    all_to_all x1, starting transfers between devices, body(): lax.all_to_all(rows.reshape(ROWS, devices, cap, width), axes, split_axis=...  7.32 us
  transfers between devices with their start and end apart: 2, of which 2 were waited for; matrix products, arithmetic and copies ran while one was open for 0% of the time, Pallas kernels for 0%

profile of v1, /device:TPU:0, one launch (start us, length us, event | category | flops | bytes accessed | tf_op | source)
XLA Modules:
  0.0 224.2 jit_solution(10733707296159244291)
XLA Ops:
  7.2 0.0 copy-start.1
  7.2 0.0 copy-start
  7.2 14.6 %shard_map.121 = f32[9,128,128]{2,1,0:T(8,128)} custom-call(s32[128]{0:T(128)} %slot_patch.1, s32[256]{0:T(256)} %patch_material.1, f32[8,64,64]{2,1,0:T(8,128)} %maps.1, f32[128,64,128]{2,1,0:T(8,128)} %state.1), custom_call_target="tpu_custom_call" | custom-call | tf_op jit(solution)/shard_map/pallas_call | solution.py:68
  21.8 2.0 copy.21
  23.8 7.3 %all-to-all-start = ((f32[9,32,4,128]{3,2,0,1:T(4,128)}), f32[9,32,4,128]{3,2,0,1:T(4,128)S(1)}, u32[]{:S(2)}, u32[]{:S(2)}) async-start(f32[9,32,4,128]{3,2,0,1:T(4,128)} %copy.21), calls=%async_computation | async-start | bytes 1179648 | tf_op jit(solution)/shard_map/all_to_all | solution.py:305
  31.1 0.0 all-reduce.3.cloned.1.call-start
  31.2 0.0 copy-done.1
  31.2 0.1 copy.19
  31.3 0.1 reshape_reshape.8.src_column
  31.4 0.1 reshape_reshape.6.src_lane
  31.5 15.2 %all-to-all-done = f32[9,32,4,128]{3,2,0,1:T(4,128)S(1)} async-done(((f32[9,32,4,128]{3,2,0,1:T(4,128)}), f32[9,32,4,128]{3,2,0,1:T(4,128)S(1)}, u32[]{:S(2)}, u32[]{:S(2)}) %all-to-all-start) | async-done | bytes 589856 | tf_op jit(solution)/shard_map/all_to_all | solution.py:305
  46.6 0.1 copy.22
  46.8 0.2 fusion.1
  46.9 0.0 copy-done
  47.0 41.4 %shard_map.122 = (f32[32,16,512]{2,1,0:T(8,128)S(1)}, f32[32,16,512]{2,1,0:T(8,128)S(1)}, f32[128,128]{1,0:T(8,128)S(1)}) custom-call(f32[32,16,512]{2,1,0:T(8,128)S(1)} %copy-done, f32[32,16,512]{2,1,0:T(8,128)} %p_prev.1, f32[32,16,512]{2,1,0:T(8,128)} %a_now.1, f32[32,16,512]{2,1,0:T(8,128)} %a_prev.1, f32[32,16,512]{2,1,0:T(8,128)} %speed2.1, ...), custom_call_target="tpu_custom_call" | custom-call | tf_op jit(solution)/shard_map/pallas_call | solution.py:267
  88.4 1.0 fusion
  89.4 0.0 all-reduce.3.cloned.1.call-update
  89.4 124.7 %all-reduce.3.cloned.1.call-done = f32[256,128]{1,0:T(8,128)} async-done(((f32[256,128]{1,0:T(8,128)}), f32[256,128]{1,0:T(8,128)}) %all-reduce.3.cloned.1.call-update) | async-done | bytes 131088
  214.2 1.3 constant_dynamic-slice_fusion
  215.4 1.0 copy.27
  216.4 1.0 copy.28
Async XLA Ops:
  7.2 24.0 %copy-start.1 = (s32[1,32,4]{1,2,0:T(4,128)S(1)}, s32[1,32,4]{1,2,0:T(4,128)}, u32[]{:S(2)}) copy-start(s32[1,32,4]{1,2,0:T(4,128)} %param.17) | copy-start | bytes 1540
  7.2 39.8 %copy-start = (f32[32,16,512]{2,1,0:T(8,128)S(1)}, f32[32,16,512]{2,1,0:T(8,128)}, u32[]{:S(2)}) copy-start(f32[32,16,512]{2,1,0:T(8,128)} %p_now.1) | copy-start | bytes 3145732
  23.8 22.8 %all-to-all-start = ((f32[9,32,4,128]{3,2,0,1:T(4,128)}), f32[9,32,4,128]{3,2,0,1:T(4,128)S(1)}, u32[]{:S(2)}, u32[]{:S(2)}) async-start(f32[9,32,4,128]{3,2,0,1:T(4,128)} %copy.21), calls=%async_computation | async-start | bytes 1179648 | tf_op jit(solution)/shard_map/all_to_all | solution.py:305
  31.1 183.0 %all-reduce.3.cloned.1.call-start = ((), (), s32[]{:S(2)}) async-start(), calls=%async_computation.1 | async-start | bytes 262144
Sparse Core Ops, SparseCore 0:
  89.5 124.5 all-reduce.2

commit v2 on v1

--- a/solution.py
+++ b/solution.py
@@ -41,7 +41,15 @@
                 h = got[1:2] * halve
                 inner.append(h)
             rows = jnp.concatenate(surface + inner, axis=0)
-            table[m] = rows
+            high = rows.astype(jnp.bfloat16)
+            low = (rows - high.astype(jnp.float32)).astype(jnp.bfloat16)
+            table[m] = jnp.concatenate(
+                [
+                    jnp.concatenate([high, high], axis=1),
+                    jnp.concatenate([low, jnp.zeros_like(low)], axis=1),
+                ],
+                axis=0,
+            )
             first = rows[:, 0:1] / (1.0 - KAPPA)
             info[m] = jnp.sum(jnp.where(row8 == lane8, first, 0.0), axis=0, keepdims=True)
 
@@ -51,10 +59,13 @@
     for i in range(block):
         patch = slot_patch[base + i]
         mat = patch_material[patch]
-        got = jnp.dot(
-            table[mat], state[i], precision=lax.Precision.HIGHEST,
-            preferred_element_type=jnp.float32,
+        start = state[i]
+        high = start.astype(jnp.bfloat16)
+        low = (start - high.astype(jnp.float32)).astype(jnp.bfloat16)
+        both = jnp.dot(
+            table[mat], jnp.concatenate([high, low], axis=0), preferred_element_type=jnp.float32
         )
+        got = both[: 2 * STEPS] + both[2 * STEPS :]
         for n in range(2 * STEPS):
             out[n, i : i + 1, :] = got[n : n + 1]
         patches = jnp.full((1, LANES), patch, jnp.int32).astype(jnp.float32)
@@ -77,7 +88,7 @@
             ],
             out_specs=pl.BlockSpec((ROWS, block, width), lambda i, *_: (0, i, 0)),
             scratch_shapes=[
-                pltpu.VMEM((mats, 2 * STEPS, depth), jnp.float32),
+                pltpu.VMEM((mats, 4 * STEPS, 2 * depth), jnp.bfloat16),
                 pltpu.VMEM((mats, 1, width), jnp.float32),
             ],
         ),
@@ -312,7 +323,10 @@
     patch = relay[ROWS - 1, :, ROWS - 1].astype(jnp.int32)
     owners = (patch[:, None] == jnp.arange(patches, dtype=jnp.int32)[None, :]).astype(jnp.float32)
     local = jnp.einsum("sp,sw->pw", owners, corr, precision=lax.Precision.HIGHEST)
-    gradient = lax.psum_scatter(local, axes, scatter_dimension=0, tiled=True)
+    parts = lax.all_to_all(
+        local.reshape(devices, patches // devices, width), axes, split_axis=0, concat_axis=0, tiled=True
+    )
+    gradient = jnp.sum(parts, axis=0)
     return pressure_out, adjoint_out, gradient
 
 

time: 225 us -> 97.9 us (0.44)
  waiting for transfers between devices: 140 us -> 23.6 us
  between operations: 14.1 us -> 0.71 us
  starting transfers between devices: 7.37 us -> 12 us
    unnamed x2 -> x0, waiting for transfers between devices: 125 us -> none
    all_to_all x0 -> x1, waiting for transfers between devices: none -> 8.38 us  [body(): lax.all_to_all(local.reshape(devices, patches // devices, width), axes, s...]
    all_to_all x0 -> x1, starting transfers between devices: none -> 4.68 us  [body(): lax.all_to_all(local.reshape(devices, patches // devices, width), axes, s...]
where the time goes in v2:
time: 97.9 us; the launch traced here: 97.5 us
  Pallas kernels  55 us (56%)
  waiting for transfers between devices  23.6 us (24%)
  starting transfers between devices  12 us (12%)
  local copies, waits for them, and re-layouts  4.31 us (4%)
  matrix products  1.01 us (1%)
    pallas_call x1, Pallas kernels, wave(): pl.pallas_call(functools.partial(wave_kernel, nx, nz), out_shape=(jax.Sha...  41.5 us
    all_to_all x1, waiting for transfers between devices, body(): lax.all_to_all(rows.reshape(ROWS, devices, cap, width), axes, split_axis=...  15.2 us
    pallas_call x1, Pallas kernels, project(): pl.pallas_call(functools.partial(project_kernel, block), out_shape=jax.Sh...  13.5 us
    all_to_all x1, waiting for transfers between devices, body(): lax.all_to_all(local.reshape(devices, patches // devices, width), axes, s...  8.38 us
    all_to_all x1, starting transfers between devices, body(): lax.all_to_all(rows.reshape(ROWS, devices, cap, width), axes, split_axis=...  7.32 us
    all_to_all x1, starting transfers between devices, body(): lax.all_to_all(local.reshape(devices, patches // devices, width), axes, s...  4.68 us
    unnamed x7, local copies, waits for them, and re-layouts  2.04 us
    reshape x1, local copies, waits for them, and re-layouts, body(): rows.reshape(ROWS, devices, cap, width)  1.98 us
  transfers between devices with their start and end apart: 2, of which 2 were waited for; matrix products, arithmetic and copies ran while one was open for 0% of the time, Pallas kernels for 0%

profile of v2, /device:TPU:0, one launch (start us, length us, event | category | flops | bytes accessed | tf_op | source)
XLA Modules:
  0.0 97.5 jit_solution(18310677380627372174)
XLA Ops:
  0.6 0.0 copy-start.1
  0.6 0.0 copy-start
  0.7 13.5 %shard_map.121 = f32[9,128,128]{2,1,0:T(8,128)} custom-call(s32[128]{0:T(128)} %slot_patch.1, s32[256]{0:T(256)} %patch_material.1, f32[8,64,64]{2,1,0:T(8,128)} %maps.1, f32[128,64,128]{2,1,0:T(8,128)} %state.1), custom_call_target="tpu_custom_call" | custom-call | tf_op jit(solution)/shard_map/pallas_call | solution.py:79
  14.2 2.0 %copy.21 = f32[9,32,4,128]{3,2,0,1:T(4,128)} copy(f32[9,32,4,128]{3,2,1,0:T(4,128)} %bitcast.7) | data formatting | bytes 1179648 | tf_op jit(solution)/shard_map/reshape | solution.py:317
  16.2 7.3 %all-to-all-start = ((f32[9,32,4,128]{3,2,0,1:T(4,128)}), f32[9,32,4,128]{3,2,0,1:T(4,128)S(1)}, u32[]{:S(2)}, u32[]{:S(2)}) async-start(f32[9,32,4,128]{3,2,0,1:T(4,128)} %copy.21), calls=%async_computation | async-start | bytes 1179648 | tf_op jit(solution)/shard_map/all_to_all | solution.py:316
  23.5 0.0 copy-done.1
  23.5 0.1 copy.19
  23.6 0.1 reshape_reshape.8.src_column
  23.7 0.1 reshape_reshape.6.src_lane
  23.8 15.2 %all-to-all-done = f32[9,32,4,128]{3,2,0,1:T(4,128)S(1)} async-done(((f32[9,32,4,128]{3,2,0,1:T(4,128)}), f32[9,32,4,128]{3,2,0,1:T(4,128)S(1)}, u32[]{:S(2)}, u32[]{:S(2)}) %all-to-all-start) | async-done | bytes 589856 | tf_op jit(solution)/shard_map/all_to_all | solution.py:316
  39.0 0.1 copy.22
  39.1 0.2 fusion
  39.3 0.0 copy-done
  39.3 41.5 %shard_map.122 = (f32[32,16,512]{2,1,0:T(8,128)S(1)}, f32[32,16,512]{2,1,0:T(8,128)S(1)}, f32[128,128]{1,0:T(8,128)S(1)}) custom-call(f32[32,16,512]{2,1,0:T(8,128)S(1)} %copy-done, f32[32,16,512]{2,1,0:T(8,128)} %p_prev.1, f32[32,16,512]{2,1,0:T(8,128)} %a_now.1, f32[32,16,512]{2,1,0:T(8,128)} %a_prev.1, f32[32,16,512]{2,1,0:T(8,128)} %speed2.1, ...), custom_call_target="tpu_custom_call" | custom-call | tf_op jit(solution)/shard_map/pallas_call | solution.py:278
  80.8 1.0 %convolution_bitcast_fusion = f32[32,8,128]{2,1,0:T(8,128)} fusion(f32[128,128]{1,0:T(8,128)S(1)} %get-tuple-element.8, s32[128]{0:T(128)S(1)} %fusion), kind=kOutput, calls=%fused_computation | convolution fusion | flops 50364416 | bytes 197120 | tf_op jit(solution)/shard_map/sp,sw->pw/dot_general | solution.py:325
  81.8 4.7 %all-to-all-start.1 = ((f32[32,8,128]{2,1,0:T(8,128)}), f32[32,8,128]{2,1,0:T(8,128)S(1)}, u32[]{:S(2)}, u32[]{:S(2)}) async-start(f32[32,8,128]{2,1,0:T(8,128)} %convolution_bitcast_fusion), calls=%async_computation.1 | async-start | bytes 262144 | tf_op jit(solution)/shard_map/all_to_all | solution.py:326
  86.5 8.4 %all-to-all-done.1 = f32[32,8,128]{2,1,0:T(8,128)S(1)} async-done(((f32[32,8,128]{2,1,0:T(8,128)}), f32[32,8,128]{2,1,0:T(8,128)S(1)}, u32[]{:S(2)}, u32[]{:S(2)}) %all-to-all-start.1) | async-done | bytes 131104 | tf_op jit(solution)/shard_map/all_to_all | solution.py:326
  94.9 0.6 reduce_sum.9
  95.5 1.0 copy.26
  96.5 1.0 copy.27
Async XLA Ops:
  0.6 22.9 %copy-start.1 = (s32[1,32,4]{1,2,0:T(4,128)S(1)}, s32[1,32,4]{1,2,0:T(4,128)}, u32[]{:S(2)}) copy-start(s32[1,32,4]{1,2,0:T(4,128)} %param.17) | copy-start | bytes 1540
  0.6 38.7 %copy-start = (f32[32,16,512]{2,1,0:T(8,128)S(1)}, f32[32,16,512]{2,1,0:T(8,128)}, u32[]{:S(2)}) copy-start(f32[32,16,512]{2,1,0:T(8,128)} %p_now.1) | copy-start | bytes 3145732
  16.2 22.8 %all-to-all-start = ((f32[9,32,4,128]{3,2,0,1:T(4,128)}), f32[9,32,4,128]{3,2,0,1:T(4,128)S(1)}, u32[]{:S(2)}, u32[]{:S(2)}) async-start(f32[9,32,4,128]{3,2,0,1:T(4,128)} %copy.21), calls=%async_computation | async-start | bytes 1179648 | tf_op jit(solution)/shard_map/all_to_all | solution.py:316
  81.8 13.1 %all-to-all-start.1 = ((f32[32,8,128]{2,1,0:T(8,128)}), f32[32,8,128]{2,1,0:T(8,128)S(1)}, u32[]{:S(2)}, u32[]{:S(2)}) async-start(f32[32,8,128]{2,1,0:T(8,128)} %convolution_bitcast_fusion), calls=%async_computation.1 | async-start | bytes 262144 | tf_op jit(solution)/shard_map/all_to_all | solution.py:326

commit v3 on v2

--- a/solution.py
+++ b/solution.py
@@ -23,24 +23,23 @@
 
     @pl.when(pl.program_id(0) == 0)
     def _():
-        @pl.loop(0, mats)
-        def _(m):
-            full = maps[m]
-            v = full[0:1, :]
-            h = jnp.zeros_like(v)
-            surface, inner = [], []
-            for n in range(STEPS):
-                dv = v * halve
-                surface.append(dv)
-                pair = jnp.concatenate([dv, v + h] + [jnp.zeros_like(v)] * 6, axis=0)
+        v = [maps[m, 0:1, :] for m in range(mats)]
+        h = [jnp.zeros_like(v[0])] * mats
+        surface, inner = [[] for _ in v], [[] for _ in v]
+        for n in range(STEPS):
+            for m in range(mats):
+                dv = v[m] * halve
+                surface[m].append(dv)
+                pair = jnp.concatenate([dv, v[m] + h[m]] + [jnp.zeros_like(dv)] * 6, axis=0)
                 got = jnp.dot(
-                    pair, full, precision=lax.Precision.HIGHEST,
+                    pair, maps[m], precision=lax.Precision.HIGHEST,
                     preferred_element_type=jnp.float32,
                 )
-                v = got[0:1]
-                h = got[1:2] * halve
-                inner.append(h)
-            rows = jnp.concatenate(surface + inner, axis=0)
+                v[m] = got[0:1]
+                h[m] = got[1:2] * halve
+                inner[m].append(h[m])
+        for m in range(mats):
+            rows = jnp.concatenate(surface[m] + inner[m], axis=0)
             high = rows.astype(jnp.bfloat16)
             low = (rows - high.astype(jnp.float32)).astype(jnp.bfloat16)
             table[m] = jnp.concatenate(
@@ -252,7 +251,7 @@
             plane(0, z_recv[step, field, 0], current[1])
             plane(cz - 1, current[cz - 2], z_recv[step, field, 1])
 
-            @pl.loop(1, cz - 1)
+            @pl.loop(1, cz - 1, unroll=2)
             def _(z):
                 plane(z, current[z - 1], current[z + 1])
 

time: 97.9 us -> 83.6 us (0.85)
  Pallas kernels: 55 us -> 40.8 us
    pallas_call x1, Pallas kernels: 41.5 us -> 32.2 us  [wave(): pl.pallas_call(functools.partial(wave_kernel, nx, nz), out_shape=(jax.Sha...]
    pallas_call x1, Pallas kernels: 13.5 us -> 8.56 us  [project(): pl.pallas_call(functools.partial(project_kernel, block), out_shape=jax.Sh...]
where the time goes in v3:
time: 83.6 us; the launch traced here: 83.2 us
  Pallas kernels  40.8 us (49%)
  waiting for transfers between devices  23.6 us (28%)
  starting transfers between devices  11.9 us (14%)
  local copies, waits for them, and re-layouts  4.31 us (5%)
  matrix products  1.01 us (1%)
    pallas_call x1, Pallas kernels, wave(): pl.pallas_call(functools.partial(wave_kernel, nx, nz), out_shape=(jax.Sha...  32.2 us
    all_to_all x1, waiting for transfers between devices, body(): lax.all_to_all(rows.reshape(ROWS, devices, cap, width), axes, split_axis=...  15.2 us
    pallas_call x1, Pallas kernels, project(): pl.pallas_call(functools.partial(project_kernel, block), out_shape=jax.Sh...  8.56 us
    all_to_all x1, waiting for transfers between devices, body(): lax.all_to_all(local.reshape(devices, patches // devices, width), axes, s...  8.38 us
    all_to_all x1, starting transfers between devices, body(): lax.all_to_all(rows.reshape(ROWS, devices, cap, width), axes, split_axis=...  7.32 us
    all_to_all x1, starting transfers between devices, body(): lax.all_to_all(local.reshape(devices, patches // devices, width), axes, s...  4.62 us
    unnamed x7, local copies, waits for them, and re-layouts  2.04 us
    reshape x1, local copies, waits for them, and re-layouts, body(): rows.reshape(ROWS, devices, cap, width)  1.98 us
  transfers between devices with their start and end apart: 2, of which 2 were waited for; matrix products, arithmetic and copies ran while one was open for 0% of the time, Pallas kernels for 0%

profile of v3, /device:TPU:0, one launch (start us, length us, event | category | flops | bytes accessed | tf_op | source)
XLA Modules:
  0.0 83.2 jit_solution(3953484588717489818)
XLA Ops:
  0.6 0.0 copy-start.1
  0.6 0.0 copy-start
  0.7 8.6 %shard_map.121 = f32[9,128,128]{2,1,0:T(8,128)} custom-call(s32[128]{0:T(128)} %slot_patch.1, s32[256]{0:T(256)} %patch_material.1, f32[8,64,64]{2,1,0:T(8,128)} %maps.1, f32[128,64,128]{2,1,0:T(8,128)} %state.1), custom_call_target="tpu_custom_call" | custom-call | tf_op jit(solution)/shard_map/pallas_call | solution.py:78
  9.2 2.0 %copy.21 = f32[9,32,4,128]{3,2,0,1:T(4,128)} copy(f32[9,32,4,128]{3,2,1,0:T(4,128)} %bitcast.7) | data formatting | bytes 1179648 | tf_op jit(solution)/shard_map/reshape | solution.py:316
  11.2 7.3 %all-to-all-start = ((f32[9,32,4,128]{3,2,0,1:T(4,128)}), f32[9,32,4,128]{3,2,0,1:T(4,128)S(1)}, u32[]{:S(2)}, u32[]{:S(2)}) async-start(f32[9,32,4,128]{3,2,0,1:T(4,128)} %copy.21), calls=%async_computation | async-start | bytes 1179648 | tf_op jit(solution)/shard_map/all_to_all | solution.py:315
  18.5 0.0 copy-done.1
  18.5 0.1 copy.19
  18.6 0.1 reshape_reshape.8.src_column
  18.7 0.1 reshape_reshape.6.src_lane
  18.8 15.2 %all-to-all-done = f32[9,32,4,128]{3,2,0,1:T(4,128)S(1)} async-done(((f32[9,32,4,128]{3,2,0,1:T(4,128)}), f32[9,32,4,128]{3,2,0,1:T(4,128)S(1)}, u32[]{:S(2)}, u32[]{:S(2)}) %all-to-all-start) | async-done | bytes 589856 | tf_op jit(solution)/shard_map/all_to_all | solution.py:315
  34.0 0.1 copy.22
  34.2 0.2 fusion
  34.3 0.0 copy-done
  34.4 32.2 %shard_map.122 = (f32[32,16,512]{2,1,0:T(8,128)S(1)}, f32[32,16,512]{2,1,0:T(8,128)S(1)}, f32[128,128]{1,0:T(8,128)S(1)}) custom-call(f32[32,16,512]{2,1,0:T(8,128)S(1)} %copy-done, f32[32,16,512]{2,1,0:T(8,128)} %p_prev.1, f32[32,16,512]{2,1,0:T(8,128)} %a_now.1, f32[32,16,512]{2,1,0:T(8,128)} %a_prev.1, f32[32,16,512]{2,1,0:T(8,128)} %speed2.1, ...), custom_call_target="tpu_custom_call" | custom-call | tf_op jit(solution)/shard_map/pallas_call | solution.py:277
  66.6 1.0 %convolution_bitcast_fusion = f32[32,8,128]{2,1,0:T(8,128)} fusion(f32[128,128]{1,0:T(8,128)S(1)} %get-tuple-element.8, s32[128]{0:T(128)S(1)} %fusion), kind=kOutput, calls=%fused_computation | convolution fusion | flops 50364416 | bytes 197120 | tf_op jit(solution)/shard_map/sp,sw->pw/dot_general | solution.py:324
  67.6 4.6 %all-to-all-start.1 = ((f32[32,8,128]{2,1,0:T(8,128)}), f32[32,8,128]{2,1,0:T(8,128)S(1)}, u32[]{:S(2)}, u32[]{:S(2)}) async-start(f32[32,8,128]{2,1,0:T(8,128)} %convolution_bitcast_fusion), calls=%async_computation.1 | async-start | bytes 262144 | tf_op jit(solution)/shard_map/all_to_all | solution.py:325
  72.2 8.4 %all-to-all-done.1 = f32[32,8,128]{2,1,0:T(8,128)S(1)} async-done(((f32[32,8,128]{2,1,0:T(8,128)}), f32[32,8,128]{2,1,0:T(8,128)S(1)}, u32[]{:S(2)}, u32[]{:S(2)}) %all-to-all-start.1) | async-done | bytes 131104 | tf_op jit(solution)/shard_map/all_to_all | solution.py:325
  80.6 0.6 reduce_sum.9
  81.2 1.0 %copy.26 = f32[32,16,512]{2,1,0:T(8,128)} copy(f32[32,16,512]{2,1,0:T(8,128)S(1)} %get-tuple-element.12) | data formatting | bytes 2097152
  82.2 1.0 %copy.27 = f32[32,16,512]{2,1,0:T(8,128)} copy(f32[32,16,512]{2,1,0:T(8,128)S(1)} %get-tuple-element.13) | data formatting | bytes 2097152
Async XLA Ops:
  0.6 17.9 %copy-start.1 = (s32[1,32,4]{1,2,0:T(4,128)S(1)}, s32[1,32,4]{1,2,0:T(4,128)}, u32[]{:S(2)}) copy-start(s32[1,32,4]{1,2,0:T(4,128)} %param.17) | copy-start | bytes 1540
  0.6 33.7 %copy-start = (f32[32,16,512]{2,1,0:T(8,128)S(1)}, f32[32,16,512]{2,1,0:T(8,128)}, u32[]{:S(2)}) copy-start(f32[32,16,512]{2,1,0:T(8,128)} %p_now.1) | copy-start | bytes 3145732
  11.2 22.8 %all-to-all-start = ((f32[9,32,4,128]{3,2,0,1:T(4,128)}), f32[9,32,4,128]{3,2,0,1:T(4,128)S(1)}, u32[]{:S(2)}, u32[]{:S(2)}) async-start(f32[9,32,4,128]{3,2,0,1:T(4,128)} %copy.21), calls=%async_computation | async-start | bytes 1179648 | tf_op jit(solution)/shard_map/all_to_all | solution.py:315
  67.6 13.0 %all-to-all-start.1 = ((f32[32,8,128]{2,1,0:T(8,128)}), f32[32,8,128]{2,1,0:T(8,128)S(1)}, u32[]{:S(2)}, u32[]{:S(2)}) async-start(f32[32,8,128]{2,1,0:T(8,128)} %convolution_bitcast_fusion), calls=%async_computation.1 | async-start | bytes 262144 | tf_op jit(solution)/shard_map/all_to_all | solution.py:325
